TPU v7x, 32 devices: a whole 2x2x4 slice. The times are simulated.
32 devices in a mesh: grp: 4 (over z), seq: 8 (over y, x, core).
Axes of the slice: x: 2, y: 2, z: 4, core: 2. Of those that a mesh axis runs over, the one named last changes fastest.
Arguments:
- tokens: bfloat16 [4096, 2048], P(('grp', 'seq')), may hold values from -6 to 6
- norm_gains: float32 [2, 2048], replicated, may hold values from 0.5 to 1.5
- norm_biases: float32 [2, 2048], replicated, may hold values from -1 to 1
- mix_weight: bfloat16 [2048, 3, 2048], P(None, None, 'seq'), may hold values from -0.125 to 0.125
- mix_bias: bfloat16 [3, 2048], P(None, 'seq'), may hold values from -1.796875 to 1.796875
- out_weight: bfloat16 [2048, 2048], P('seq'), may hold values from -0.5 to 0.5
- gate_up_weight: bfloat16 [2048, 2, 5632], P(None, None, 'seq'), may hold values from -0.125 to 0.125
- down_weight: bfloat16 [5632, 2048], P('seq'), may hold values from -0.078125 to 0.078125
- row_lengths: int32 [8], replicated, may hold values from 128 to 1024, as said below
- row_group: int32 [8], replicated, may hold values from 0 to 3, as said below
- cotangent: bfloat16 [4096, 2048], P(('grp', 'seq')), may hold values from -6 to 6
Outputs:
- layer_out: bfloat16 [4096, 2048], P(('grp', 'seq'))
- tokens_grad: bfloat16 [4096, 2048], P(('grp', 'seq'))
- gains_grad: float32 [2, 2048], replicated
- biases_grad: float32 [2, 2048], replicated
- mix_grad: float32 [2048, 3, 2048], P(None, None, 'seq')
- mix_bias_grad: float32 [3, 2048], P(None, 'seq')
- out_grad: float32 [2048, 2048], P('seq')
- gate_up_grad: float32 [2048, 2, 5632], P(None, None, 'seq')
- down_grad: float32 [5632, 2048], P('seq')
Inputs may be any that keep to these rules, and one draw needn't show every extreme that they name: `row_lengths`: rows 0 to 1 are 1024 long; every other row's length is a multiple of 128 and at most 256. `row_group`: each of rows 0 to 1 fills a group alone; every other group holds exactly three of the other rows.
All inputs are finite; a program needn't handle non-finite values.
Results may differ from a plain program's by a relative error of at most 0.02.
Values may be sent and summed in bfloat16 or wider, within the bound.
A program may use at most 320 MiB of HBM per device.

v0:
```python
import math
import jax
import jax.numpy as jnp
from jax import lax
from jax.sharding import PartitionSpec as P

HEAD_DIM = 64
ROT = 16
EPS = 1e-05
NEG = -1e30
BASE = 10000.0


def layer_norm(values, gain, bias):
    centered = values - jnp.mean(values, axis=-1, keepdims=True)
    scale = lax.rsqrt(jnp.mean(centered * centered, axis=-1, keepdims=True) + EPS)
    unit = centered * scale
    return (unit * gain + bias, unit, scale)


def norm_back(incoming, unit, scale, gain):
    along = incoming * gain
    inner = jnp.mean(along, axis=-1, keepdims=True)
    cross = jnp.mean(along * unit, axis=-1, keepdims=True)
    return (
        scale * (along - inner - unit * cross),
        jnp.sum(incoming * unit, axis=0),
        jnp.sum(incoming, axis=0),
    )


def rotate(values, where, sign):
    half = ROT // 2
    freq = BASE ** (-jnp.arange(half, dtype=jnp.float32) / half)
    angle = where.astype(jnp.float32)[:, None] * freq[None, :]
    cosine = jnp.cos(angle)[:, None, :]
    sine = sign * jnp.sin(angle)[:, None, :]
    first = values[..., :half]
    second = values[..., half:ROT]
    return jnp.concatenate(
        [first * cosine - second * sine, second * cosine + first * sine, values[..., ROT:]], axis=-1
    )


def unrotate(lowered, where):
    wide = lowered.astype(jnp.float32)
    turned = jnp.stack(
        [rotate(wide[:, 0], where, -1.0), rotate(wide[:, 1], where, -1.0), wide[:, 2]], axis=1
    )
    return turned.reshape(lowered.shape[0], 3, -1).astype(jnp.bfloat16)


def slot_rows(row_lengths, row_group, group, slots):
    order = jnp.arange(row_lengths.shape[0], dtype=jnp.int32)
    same = row_group == group
    earlier = (order[:, None] > order[None, :]) & same[None, :]
    begin = jnp.sum(jnp.where(earlier, row_lengths[None, :], 0), axis=1)
    finish = begin + row_lengths
    inside = same[None, :] & (slots[:, None] >= begin[None, :]) & (slots[:, None] < finish[None, :])
    label = jnp.sum(jnp.where(inside, order[None, :] + 1, 0), axis=1) - 1
    offset = jnp.sum(jnp.where(inside, slots[:, None] - begin[None, :], 0), axis=1)
    load = jnp.sum(jnp.where(same, row_lengths, 0))
    return (label, jnp.where(label < 0, slots - load, offset))


def block_scores(query, key, label, start, block):
    part = lax.dynamic_slice_in_dim(query, start, block, 0)
    rows = start + jnp.arange(block, dtype=jnp.int32)
    columns = jnp.arange(label.shape[0], dtype=jnp.int32)
    label_rows = lax.dynamic_slice_in_dim(label, start, block, 0)
    allowed = (label_rows[:, None] == label[None, :]) & (rows[:, None] >= columns[None, :])
    scores = jnp.einsum("qhe,khe->hqk", part, key, preferred_element_type=jnp.float32) * (
        1.0 / math.sqrt(query.shape[-1])
    )
    return (part, jnp.where(allowed[None], scores, NEG))


def attend(query, key, value, label, block):

    def one_block(index):
        part, scores = block_scores(query, key, label, index * block, block)
        top = jnp.max(scores, axis=-1, keepdims=True)
        weights = jnp.exp(scores - top)
        totals = jnp.sum(weights, axis=-1, keepdims=True)
        probs = (weights / totals).astype(jnp.bfloat16)
        mixed = jnp.einsum("hqk,khe->qhe", probs, value, preferred_element_type=jnp.float32)
        return (mixed, top[..., 0] + jnp.log(totals[..., 0]))

    mixed, log_totals = lax.map(one_block, jnp.arange(query.shape[0] // block, dtype=jnp.int32))
    return (mixed.reshape(query.shape), log_totals)


def attend_back(query, key, value, label, log_totals, mixed_back, block):
    scale = 1.0 / math.sqrt(query.shape[-1])

    def one_block(carry, index):
        key_back, value_back = carry
        start = index * block
        part, scores = block_scores(query, key, label, start, block)
        back_part = lax.dynamic_slice_in_dim(mixed_back, start, block, 0)
        probs = jnp.exp(scores - log_totals[index][..., None])
        value_back = value_back + jnp.einsum(
            "hqk,qhe->khe",
            probs.astype(jnp.bfloat16),
            back_part,
            preferred_element_type=jnp.float32,
        )
        probs_back = jnp.einsum(
            "qhe,khe->hqk", back_part, value, preferred_element_type=jnp.float32
        )
        inner = jnp.sum(probs_back * probs, axis=-1, keepdims=True)
        score_back = (probs * (probs_back - inner)).astype(jnp.bfloat16)
        query_back = (
            jnp.einsum("hqk,khe->qhe", score_back, key, preferred_element_type=jnp.float32) * scale
        )
        key_back = (
            key_back
            + jnp.einsum("hqk,qhe->khe", score_back, part, preferred_element_type=jnp.float32)
            * scale
        )
        return ((key_back, value_back), query_back)

    empty = jnp.zeros(key.shape, jnp.float32)
    (key_back, value_back), query_back = lax.scan(
        one_block, (empty, empty), jnp.arange(query.shape[0] // block, dtype=jnp.int32)
    )
    return (query_back.reshape(query.shape), key_back, value_back)


def silu_parts(gate_up):
    gate = gate_up[:, 0]
    upper = gate_up[:, 1]
    sigma = jax.nn.sigmoid(gate)
    return (gate * sigma * upper, gate, upper, sigma)


def gate_back(hidden_back, gate, upper, sigma):
    gate_part = hidden_back * upper * sigma * (1.0 + gate * (1.0 - sigma))
    up_part = hidden_back * gate * sigma
    return jnp.stack([gate_part, up_part], axis=1).astype(jnp.bfloat16)


def gather_rows(values):
    return lax.all_gather(values, "seq", axis=0, tiled=True)


def summed_rows(product, left):
    return lax.psum_scatter(
        product(left).astype(jnp.bfloat16), "seq", scatter_dimension=0, tiled=True
    ).astype(jnp.float32)


def on_device(
    tokens,
    norm_gains,
    norm_biases,
    mix_weight,
    mix_bias,
    out_weight,
    gate_up_weight,
    down_weight,
    row_lengths,
    row_group,
    cotangent,
):
    seq_count = lax.axis_size("seq")
    shard = lax.axis_index("seq")
    group = lax.axis_index("grp")
    slots_dev = tokens.shape[0]
    width = tokens.shape[1]
    group_slots = slots_dev * seq_count
    block = min(512, group_slots)
    local_width = width // seq_count
    local_heads = local_width // HEAD_DIM
    mine = shard * slots_dev + jnp.arange(slots_dev, dtype=jnp.int32)
    label_mine, place_mine = slot_rows(row_lengths, row_group, group, mine)
    label_all, place_all = slot_rows(
        row_lengths, row_group, group, jnp.arange(group_slots, dtype=jnp.int32)
    )
    inputs = tokens.astype(jnp.float32)
    upstream = cotangent.astype(jnp.float32) * (label_mine >= 0).astype(jnp.float32)[:, None]
    upstream_low = upstream.astype(jnp.bfloat16)
    normed, unit_one, scale_one = layer_norm(inputs, norm_gains[0], norm_biases[0])
    normed_low = normed.astype(jnp.bfloat16)
    mix_full, bias_full, out_full = (
        lax.all_gather(mix_weight, "seq", axis=2, tiled=True),
        lax.all_gather(mix_bias, "seq", axis=1, tiled=True),
        lax.all_gather(out_weight, "seq", axis=0, tiled=True),
    )
    mixin = jnp.einsum(
        "td,dcf->tcf", normed_low, mix_full, preferred_element_type=jnp.float32
    ) + bias_full.astype(jnp.float32)
    heads_in = mixin.reshape(slots_dev, 3, width // HEAD_DIM, HEAD_DIM)
    sending = jnp.stack(
        [
            rotate(heads_in[:, 0], place_mine, 1.0),
            rotate(heads_in[:, 1], place_mine, 1.0),
            heads_in[:, 2],
        ],
        axis=1,
    ).astype(jnp.bfloat16)
    arrived = lax.all_to_all(
        sending.reshape(slots_dev, 3, seq_count, local_width),
        "seq",
        split_axis=2,
        concat_axis=0,
        tiled=True,
    )
    arrived = arrived.reshape(group_slots, 3, local_heads, HEAD_DIM)
    query, key, value = (arrived[:, 0], arrived[:, 1], arrived[:, 2])
    mixed, log_totals = attend(query, key, value, label_all, block)
    attended = lax.all_to_all(
        mixed.reshape(group_slots, local_width).astype(jnp.bfloat16),
        "seq",
        split_axis=0,
        concat_axis=1,
        tiled=True,
    )
    resid = inputs + jnp.dot(attended, out_full, preferred_element_type=jnp.float32)
    normed_two, unit_two, scale_two = layer_norm(resid, norm_gains[1], norm_biases[1])
    normed_two_all = gather_rows(normed_two.astype(jnp.bfloat16))
    gate_up = jnp.einsum(
        "td,dcf->tcf", normed_two_all, gate_up_weight, preferred_element_type=jnp.float32
    )
    hidden, gate, upper, sigma = silu_parts(gate_up)
    hidden_low = hidden.astype(jnp.bfloat16)

    def down_product(part):
        return jnp.dot(part, down_weight, preferred_element_type=jnp.float32)

    layer_out = resid + summed_rows(down_product, hidden_low)
    upstream_all = gather_rows(upstream_low)
    down_shard = jnp.einsum(
        "tf,td->fd", hidden_low, upstream_all, preferred_element_type=jnp.float32
    )
    hidden_back = jnp.einsum(
        "td,fd->tf", upstream_all, down_weight, preferred_element_type=jnp.float32
    )
    gate_up_back = gate_back(hidden_back, gate, upper, sigma)
    gate_up_shard = jnp.einsum(
        "td,tcf->dcf", normed_two_all, gate_up_back, preferred_element_type=jnp.float32
    )

    def gate_up_product(part):
        return jnp.einsum("tcf,dcf->td", part, gate_up_weight, preferred_element_type=jnp.float32)

    normed_two_back = summed_rows(gate_up_product, gate_up_back)
    resid_part, gain_two, bias_two = norm_back(normed_two_back, unit_two, scale_two, norm_gains[1])
    resid_back = upstream + resid_part
    branch_low = resid_back.astype(jnp.bfloat16)
    out_term = jnp.einsum("te,td->ed", attended, branch_low, preferred_element_type=jnp.float32)
    attended_back = jnp.einsum(
        "td,ed->te", branch_low, out_full, preferred_element_type=jnp.float32
    ).astype(jnp.bfloat16)
    heads_back = lax.all_to_all(
        attended_back, "seq", split_axis=1, concat_axis=0, tiled=True
    ).reshape(group_slots, local_heads, HEAD_DIM)
    query_back, key_back, value_back = attend_back(
        query, key, value, label_all, log_totals, heads_back, block
    )
    lowered = (
        jnp.stack([query_back, key_back, value_back], axis=1)
        .astype(jnp.bfloat16)
        .reshape(group_slots, 3, 1, local_width)
    )
    returned = lax.all_to_all(lowered, "seq", split_axis=0, concat_axis=2, tiled=True).reshape(
        slots_dev, 3, width // HEAD_DIM, HEAD_DIM
    )
    mixin_back = unrotate(returned, place_mine)
    mix_term = jnp.einsum("td,tcf->dcf", normed_low, mixin_back, preferred_element_type=jnp.float32)
    bias_term = jnp.sum(mixin_back, axis=0, dtype=jnp.float32)
    normed_back = jnp.einsum(
        "tcf,dcf->td", mixin_back, mix_full, preferred_element_type=jnp.float32
    )
    mix_shard, bias_shard, out_shard = (
        lax.psum_scatter(
            mix_term.astype(jnp.bfloat16), "seq", scatter_dimension=2, tiled=True
        ).astype(jnp.float32),
        lax.psum_scatter(
            bias_term.astype(jnp.bfloat16), "seq", scatter_dimension=1, tiled=True
        ).astype(jnp.float32),
        lax.psum_scatter(
            out_term.astype(jnp.bfloat16), "seq", scatter_dimension=0, tiled=True
        ).astype(jnp.float32),
    )
    tokens_part, gain_one, bias_one = norm_back(normed_back, unit_one, scale_one, norm_gains[0])
    tokens_grad = (resid_back + tokens_part).astype(jnp.bfloat16)
    mix_grad, mix_bias_grad, out_grad, gate_up_grad, down_grad = (
        lax.psum(mix_shard.astype(jnp.bfloat16), "grp").astype(jnp.float32),
        lax.psum(bias_shard.astype(jnp.bfloat16), "grp").astype(jnp.float32),
        lax.psum(out_shard.astype(jnp.bfloat16), "grp").astype(jnp.float32),
        lax.psum(gate_up_shard.astype(jnp.bfloat16), "grp").astype(jnp.float32),
        lax.psum(down_shard.astype(jnp.bfloat16), "grp").astype(jnp.float32),
    )
    gains_grad, biases_grad = lax.psum(
        (jnp.stack([gain_one, gain_two]), jnp.stack([bias_one, bias_two])), ("grp", "seq")
    )
    return (
        layer_out.astype(jnp.bfloat16),
        tokens_grad,
        gains_grad,
        biases_grad,
        mix_grad,
        mix_bias_grad,
        out_grad,
        gate_up_grad,
        down_grad,
    )


def solution(mesh):
    placed = (
        P(("grp", "seq"), None),
        P(),
        P(),
        P(None, None, "seq"),
        P(None, "seq"),
        P("seq", None),
        P(None, None, "seq"),
        P("seq", None),
        P(),
        P(),
        P(("grp", "seq"), None),
    )
    return jax.shard_map(
        on_device,
        mesh=mesh,
        in_specs=placed,
        out_specs=(
            P(("grp", "seq"), None),
            P(("grp", "seq"), None),
            P(),
            P(),
            P(None, None, "seq"),
            P(None, "seq"),
            P("seq", None),
            P(None, None, "seq"),
            P("seq", None),
        ),
        check_vma=False,
    )
```

profile of v0, /device:TPU:0, one launch (start us, length us, event | category | flops | bytes accessed | tf_op | source)
XLA Modules:
  0.0 1248.3 jit_solution(738130817734868844)
XLA Ops:
  9.5 10.4 all_gather.16
  21.9 121.0 %all-gather.5.cloned.1.call-done = bf16[2048,3,2048]{2,0,1:T(8,128)(2,1)} async-done(((bf16[2048,3,256]{2,0,1:T(8,128)(2,1)}), bf16[2048,3,2048]{2,0,1:T(8,128)(2,1)}) %all-gather.5.cloned.1.call-update) | async-done | bytes 25165840 | tf_op jit(solution)/shard_map/all_gather | solution.py:186
  143.0 13.4 %convolution_add_fusion = f32[128,3,2048]{2,0,1:T(8,128)} fusion(bf16[2048,3,2048]{2,0,1:T(8,128)(2,1)} %all-gather.5.cloned.1.call-done, f32[3,2048]{1,0:T(4,128)S(1)} %convert_element_type.139, bf16[128,2048]{1,0:T(8,128)(2,1)S(1)} %copy-done.5, f32[2048]{0:T(1024)S(1)} %bitcast.195, f32[2048]{0:T(1024)S(1)} %bitcast.191, f32[128]{0:T(128)S(1)} %add_rsqrt_fusion.1, ...), kind=kOutput, calls=%fused_computation.63 | convolution fusion | flops 3223584768 | bytes 28877824 | tf_op jit(solution)/shard_map/td,dcf->tcf/dot_general | solution.py:190
  156.4 3.5 copy.90
  164.7 4.5 all-to-all-start
  169.3 35.6 %all-to-all-done = bf16[128,3,8,256]{0,3,1,2:T(8,128)(2,1)} async-done(((bf16[128,3,8,256]{0,3,1,2:T(8,128)(2,1)}), bf16[128,3,8,256]{0,3,1,2:T(8,128)(2,1)}, u32[]{:S(2)}, u32[]{:S(2)}) %all-to-all-start) | async-done | bytes 1572896 | tf_op jit(solution)/shard_map/all_to_all | solution.py:202
  204.9 3.6 copy.92
  208.5 3.7 reshape.381
  212.2 2.6 slice_bitcast_fusion.6
  215.6 21.5 %while.27 = (s32[]{:T(128)}, bf16[2,512,4,64]{1,3,2,0:T(8,128)(2,1)}, f32[2,4,512]{2,1,0:T(4,128)S(1)}, s32[2]{0:T(128)S(1)}, s32[1024]{0:T(1024)S(1)}, /*index=...) while((s32[]{:T(128)}, ...), condition=%wide.region_10.11_spmd, body=%wide.region_7.10_spmd.sunk | while | flops 563608064 | bytes 35469596 | solution.py:89
  217.5 2.6 fusion.126
  220.1 2.3 fusion.127
  222.5 3.0 fusion.128
  228.2 2.6 fusion.126
  230.9 2.3 fusion.127
  233.3 3.0 fusion.128
  237.1 2.4 copy.93
  239.5 2.2 convert_element_type.142
  241.6 1.9 copy.94
  243.5 4.2 all-to-all-start.1
  247.8 9.7 all-to-all-done.1
  257.4 4.9 fusion.81
  264.5 2.0 fusion.66
  266.9 33.4 %all-gather.9.cloned.1.call-done = bf16[1024,2048]{1,0:T(8,128)(2,1)} async-done(((bf16[128,2048]{1,0:T(8,128)(2,1)}), bf16[1024,2048]{1,0:T(8,128)(2,1)}) %all-gather.9.cloned.1.call-update) | async-done | bytes 4194320 | tf_op jit(solution)/shard_map/all_gather | solution.py:144
  300.4 11.0 fusion.39
  311.4 28.1 %all-gather.11.cloned.1.call-done = bf16[1024,2048]{1,0:T(8,128)(2,1)} async-done(((bf16[128,2048]{1,0:T(8,128)(2,1)}), bf16[1024,2048]{1,0:T(8,128)(2,1)}) %all-gather.11.cloned.1.call-update) | async-done | bytes 4194320 | tf_op jit(solution)/shard_map/all_gather | solution.py:144
  339.5 8.3 fusion.45
  349.4 11.0 bitcast_convert_fusion
  360.4 6.4 convolution_convert_fusion.3
  366.9 45.0 %reduce-scatter.10.cloned.1.call-done = bf16[128,2048]{1,0:T(8,128)(2,1)} async-done(((bf16[1024,2048]{1,0:T(8,128)(2,1)}), bf16[128,2048]{1,0:T(8,128)(2,1)}) %reduce-scatter.10.cloned.1.call-update) | async-done | bytes 524304 | tf_op jit(solution)/shard_map/reduce_scatter | solution.py:148
  411.9 2.1 fusion.65
  414.0 53.4 %reduce-scatter.8.cloned.1.call-done = bf16[128,2048]{1,0:T(8,128)(2,1)} async-done(((bf16[1024,2048]{1,0:T(8,128)(2,1)}), bf16[128,2048]{1,0:T(8,128)(2,1)}) %reduce-scatter.8.cloned.1.call-update) | async-done | bytes 524304 | tf_op jit(solution)/shard_map/reduce_scatter | solution.py:148
  467.3 2.3 fusion.63
  469.7 7.1 convolution_convert_fusion.1
  476.8 6.3 convolution_convert_fusion.5
  484.0 3.5 all-to-all-start.2
  487.7 9.4 all-to-all-done.2
  498.2 2.1 reshape.382
  501.1 31.6 %while.28 = (s32[]{:T(128)}, f32[1024,4,64]{0,2,1:T(8,128)S(1)}, f32[1024,4,64]{0,2,1:T(8,128)}, bf16[2,512,4,64]{1,3,2,0:T(8,128)(2,1)}, s32[2]{0:T(128)S(1)}, ...) while((s32[]{:T(128)}, f32[1024,4,64]{0,2,1:T(8,128)S(1)}, ...), condition=%wide.region_19.20_spmd.clone, body=%wide.region_17.19_spmd.clone.sunk | while | flops 1376647680 | bytes 87103920 | solution.py:124
  506.4 2.5 fusion.141
  508.9 3.2 multiply_reduce_fusion.4
  512.1 2.4 multiply_convert_fusion.5
  522.2 2.6 fusion.141
  524.7 3.2 multiply_reduce_fusion.4
  527.9 2.4 multiply_convert_fusion.5
  532.8 1.7 copy.97
  537.6 3.0 copy.98
  540.5 29.5 %all_to_all.56 = bf16[1024,3,1,256]{3,1,2,0:T(4,128)(2,1)S(1)} all-to-all(bf16[1024,3,1,256]{3,1,2,0:T(4,128)(2,1)S(1)} %copy.98), channel_id=1, replica_groups=mesh['grp'=4,'seq'=8] {'seq'}, dimensions={0} | all-to-all | bytes 3145728 | tf_op jit(solution)/shard_map/all_to_all | solution.py:266
  571.4 1.9 copy.100
  573.4 2.1 convert_element_type.158
  575.7 1.7 slice_bitcast_fusion.3
  578.5 12.0 convolution_convert_fusion
  590.6 10.8 convolution_convert_fusion.2
  603.1 8.9 convolution_convert_fusion.4
  612.0 134.7 %reduce-scatter.12.cloned.1.call-done = bf16[2048,3,256]{2,0,1:T(8,128)(2,1)} async-done(((bf16[2048,3,2048]{2,0,1:T(8,128)(2,1)}), bf16[2048,3,256]{2,0,1:T(8,128)(2,1)}) %reduce-scatter.12.cloned.1.call-update) | async-done | bytes 3145744 | tf_op jit(solution)/shard_map/reduce_scatter | solution.py:276
  746.7 14.6 %fusion.59 = (f32[2048]{0:T(1024)S(1)}, f32[128]{0:T(128)S(1)}, f32[128]{0:T(128)S(1)}, f32[2048]{0:T(1024)S(1)}, f32[128,2048]{1,0:T(8,128)}) fusion(bf16[128,2048]{1,0:T(8,128)(2,1)S(1)} %copy-done.6, f32[128]{0:T(128)S(1)} %copy-done.35, f32[128]{0:T(128)S(1)} %copy-done.33, f32[2048]{0:T(1024)S(1)} %bitcast.193, ...), kind=kOutput, calls=%fused_computation.93 | convolution fusion | flops 3225415680 | bytes 28338176 | tf_op jit(solution)/shard_map/tcf,dcf->td/dot_general | solution.py:272
  761.4 40.2 %all-reduce = (f32[2,2048]{1,0:T(2,128)}, f32[2,2048]{1,0:T(2,128)}) all-reduce(f32[2,2048]{1,0:T(2,128)S(1)} %pad_maximum_fusion.10, f32[2,2048]{1,0:T(2,128)S(1)} %pad_maximum_fusion.11), channel_id=1, replica_groups=mesh['grp'=4,'seq'=8] {'grp','seq'}, use_global_device_ids=true, to_apply=%region_24.25 | all-reduce | flops 8192 | bytes 65536 | tf_op jit(solution)/shard_map/psum | solution.py:295
  801.6 2.5 fusion.58
  805.0 12.3 psum.52
  817.9 407.1 %all-reduce.4.cloned.1.call-done = (bf16[2048,3,256]{2,0,1:T(8,128)(2,1)}, bf16[256,2048]{1,0:T(8,128)(2,1)}, bf16[2048,2,704]{0,2,1:T(8,128)(2,1)}, bf16[704,2048]{1,0:T(8,128)(2,1)}) async-done(((bf16[2048,3,256]{2,0,1:T(8,128)(2,1)}, bf16[256,2048]{1,0:T(8,128)(2,1)}, bf16[2048,2,704]{0,2,1:T(8,128)(2,1)}, bf16[704,2048]{1,0:T(8,128)(2,1)}), (bf16[2048,3,256]{2,0,1:T(8,128)(2,1)}, ...) | async-done | bytes 12845072 | tf_op jit(solution)/shard_map/psum | solution.py:289
  1225.0 2.9 convert_element_type.164
  1228.0 3.7 convert_element_type.161
  1231.7 3.3 convert_element_type.168
  1235.0 6.0 convert_element_type.166
  (216 shorter events, 40.4 us)
Async XLA Ops:
  7.2 332.3 %copy-start = (bf16[704,2048]{1,0:T(8,128)(2,1)S(1)}, bf16[704,2048]{1,0:T(8,128)(2,1)}, u32[]{:S(2)}) copy-start(bf16[704,2048]{1,0:T(8,128)(2,1)} %param.22) | copy-start | bytes 8650756
  7.2 1.6 copy-start.38
  7.2 1.6 copy-start.37
  7.2 2.3 copy-start.36
  7.2 12.8 %copy-start.5 = (bf16[128,2048]{1,0:T(8,128)(2,1)S(1)}, bf16[128,2048]{1,0:T(8,128)(2,1)}, u32[]{:S(2)}) copy-start(bf16[128,2048]{1,0:T(8,128)(2,1)} %param.15) | copy-start | bytes 1572868
  7.2 14.6 %copy-start.30 = (f32[2,2048]{1,0:T(2,128)S(1)}, f32[2,2048]{1,0:T(2,128)}, u32[]{:S(2)}) copy-start(f32[2,2048]{1,0:T(2,128)} %param.16) | copy-start | bytes 49156
  7.2 14.6 %copy-start.31 = (f32[2,2048]{1,0:T(2,128)S(1)}, f32[2,2048]{1,0:T(2,128)}, u32[]{:S(2)}) copy-start(f32[2,2048]{1,0:T(2,128)} %param.17) | copy-start | bytes 49156
  7.3 135.7 %all-gather.5.cloned.1.call-start = ((), (), s32[]{:S(2)}) async-start(), calls=%async_computation.9 | async-start | bytes 28311552 | tf_op jit(solution)/shard_map/all_gather | solution.py:186
  8.0 239.8 %all-gather.7.cloned.1.call-start = ((), (), s32[]{:S(2)}) async-start(), calls=%async_computation.10 | async-start | bytes 9437184 | tf_op jit(solution)/shard_map/all_gather | solution.py:188
  20.2 136.2 %copy-start.32 = (f32[128]{0:T(128)}, f32[128]{0:T(128)S(1)}, u32[]{:S(2)}) copy-start(f32[128]{0:T(128)S(1)} %broadcast_multiply_fusion.6) | copy-start | bytes 1540
  20.5 135.9 %copy-start.34 = (f32[128]{0:T(128)}, f32[128]{0:T(128)S(1)}, u32[]{:S(2)}) copy-start(f32[128]{0:T(128)S(1)} %add_rsqrt_fusion.1) | copy-start | bytes 1540
  21.9 141.2 %copy-start.25 = (f32[128,8]{0,1:T(8,128)}, f32[128,8]{0,1:T(8,128)S(1)}, u32[]{:S(2)}) copy-start(f32[128,8]{0,1:T(8,128)S(1)} %get-tuple-element.253) | copy-start | bytes 12292
  21.9 134.5 %copy-start.21 = (f32[1,2048]{1,0:T(1,128)}, f32[1,2048]{1,0:T(1,128)S(1)}, u32[]{:S(2)}) copy-start(f32[1,2048]{1,0:T(1,128)S(1)} %get-tuple-element.244) | copy-start | bytes 24580
  21.9 134.4 %copy-start.23 = (f32[1,2048]{1,0:T(1,128)}, f32[1,2048]{1,0:T(1,128)S(1)}, u32[]{:S(2)}) copy-start(f32[1,2048]{1,0:T(1,128)S(1)} %get-tuple-element.246) | copy-start | bytes 24580
  164.7 40.2 %all-to-all-start = ((bf16[128,3,8,256]{0,3,1,2:T(8,128)(2,1)}), bf16[128,3,8,256]{0,3,1,2:T(8,128)(2,1)}, u32[]{:S(2)}, u32[]{:S(2)}) async-start(bf16[128,3,8,256]{0,3,1,2:T(8,128)(2,1)} %copy.91), calls=%async_computation | async-start | bytes 3145728 | tf_op jit(solution)/shard_map/all_to_all | solution.py:202
  220.1 2.4 copy-start.7
  220.1 2.4 copy-start.16
  225.5 0.8 copy-start.17
  230.9 2.4 copy-start.7
  230.9 2.4 copy-start.16
  236.3 0.8 copy-start.17
  243.5 13.9 %all-to-all-start.1 = ((bf16[8,128,256]{1,2,0:T(8,128)(2,1)}), bf16[8,128,256]{1,2,0:T(8,128)(2,1)}, u32[]{:S(2)}, u32[]{:S(2)}) async-start(bf16[8,128,256]{1,2,0:T(8,128)(2,1)} %copy.94), calls=%async_computation.1 | async-start | bytes 1048576 | tf_op jit(solution)/shard_map/all_to_all | solution.py:212
  247.7 52.7 %all-gather.9.cloned.1.call-start = ((), (), s32[]{:S(2)}) async-start(), calls=%async_computation.11 | async-start | bytes 4718592 | tf_op jit(solution)/shard_map/all_gather | solution.py:144
  262.4 1.0 copy-start.3
  264.4 75.0 %all-gather.11.cloned.1.call-start = ((), (), s32[]{:S(2)}) async-start(), calls=%async_computation.13 | async-start | bytes 4718592 | tf_op jit(solution)/shard_map/all_gather | solution.py:144
  266.5 145.4 %reduce-scatter.10.cloned.1.call-start = ((), (), s32[]{:S(2)}) async-start(), calls=%async_computation.14 | async-start | bytes 4718592 | tf_op jit(solution)/shard_map/reduce_scatter | solution.py:148
  347.8 1.1 copy-start.39
  347.8 1.6 copy-start.40
  360.4 107.0 %reduce-scatter.8.cloned.1.call-start = ((), (), s32[]{:S(2)}) async-start(), calls=%async_computation.12 | async-start | bytes 4718592 | tf_op jit(solution)/shard_map/reduce_scatter | solution.py:148
  366.8 45.0 %copy-start.4 = (f32[128,2048]{1,0:T(8,128)S(1)}, f32[128,2048]{1,0:T(8,128)}, u32[]{:S(2)}) copy-start(f32[128,2048]{1,0:T(8,128)} %copy-done.3) | copy-start | bytes 3145732
  366.8 100.5 %copy-start.18 = (bf16[128,2048]{1,0:T(8,128)(2,1)S(1)}, bf16[128,2048]{1,0:T(8,128)(2,1)}, u32[]{:S(2)}) copy-start(bf16[128,2048]{1,0:T(8,128)(2,1)} %param.25) | copy-start | bytes 1572868
  366.9 245.1 %reduce-scatter.14.cloned.1.call-start = ((), (), s32[]{:S(2)}) async-start(), calls=%async_computation.16 | async-start | bytes 9437184 | tf_op jit(solution)/shard_map/reduce_scatter | solution.py:282
  469.7 7.2 copy-start.9
  483.1 18.0 %copy-start.2 = (bf16[1024,4,64]{0,2,1:T(8,128)(2,1)S(1)}, bf16[1024,4,64]{0,2,1:T(8,128)(2,1)}, u32[]{:S(2)}) copy-start(bf16[1024,4,64]{0,2,1:T(8,128)(2,1)} %get-tuple-element.490) | copy-start | bytes 1572868
  483.1 18.0 %copy-start.8 = (bf16[1024,4,64]{0,2,1:T(8,128)(2,1)S(1)}, bf16[1024,4,64]{0,2,1:T(8,128)(2,1)}, u32[]{:S(2)}) copy-start(bf16[1024,4,64]{0,2,1:T(8,128)(2,1)} %get-tuple-element.491) | copy-start | bytes 1572868
  484.0 13.2 %all-to-all-start.2 = ((bf16[128,8,256]{2,0,1:T(8,128)(2,1)}), bf16[128,8,256]{2,0,1:T(8,128)(2,1)S(1)}, u32[]{:S(2)}, u32[]{:S(2)}) async-start(bf16[128,8,256]{2,0,1:T(8,128)(2,1)} %bitcast.142), calls=%async_computation.4 | async-start | bytes 1048576 | tf_op jit(solution)/shard_map/all_to_all | solution.py:255
  487.5 259.2 %reduce-scatter.12.cloned.1.call-start = ((), (), s32[]{:S(2)}) async-start(), calls=%async_computation.15 | async-start | bytes 28311552 | tf_op jit(solution)/shard_map/reduce_scatter | solution.py:276
  505.0 1.3 copy-start.11
  505.0 1.4 copy-start.19
  508.9 3.2 copy-start.20
  512.1 2.4 copy-start.14
  515.9 1.0 copy-start.15
  520.8 1.3 copy-start.11
  520.8 1.4 copy-start.19
  524.7 3.2 copy-start.20
  527.9 2.4 copy-start.14
  531.7 1.0 copy-start.15
  575.4 2.1 copy-start.26
  575.4 2.1 copy-start.29
  577.4 1.0 copy-start.6
  577.4 1.0 copy-start.22
  577.4 1.0 copy-start.24
  577.4 1.0 copy-start.33
  577.4 1.0 copy-start.35
  590.5 213.5 %reduce-scatter.16.cloned.1.call-start = ((), (), s32[]{:S(2)}) async-start(), calls=%async_computation.17 | async-start | bytes 589824
  602.8 622.3 %all-reduce.4.cloned.1.call-start = ((), (), s32[]{:S(2)}) async-start(), calls=%async_computation.18 | async-start | bytes 25690112 | tf_op jit(solution)/shard_map/psum | solution.py:289
  746.7 14.7 %copy-start.28 = (f32[2048]{0:T(1024)S(1)}, f32[2048]{0:T(1024)}, u32[]{:S(2)}) copy-start(f32[2048]{0:T(1024)} %get-tuple-element.165) | copy-start | bytes 24580
  746.7 14.7 %copy-start.27 = (f32[2048]{0:T(1024)S(1)}, f32[2048]{0:T(1024)}, u32[]{:S(2)}) copy-start(f32[2048]{0:T(1024)} %get-tuple-element.170) | copy-start | bytes 24580
  746.7 54.9 %copy-start.10 = (f32[128,2048]{1,0:T(8,128)S(1)}, f32[128,2048]{1,0:T(8,128)}, u32[]{:S(2)}) copy-start(f32[128,2048]{1,0:T(8,128)} %copy-done.9) | copy-start | bytes 3145732
  1225.0 2.9 copy-start.12
  1225.0 10.0 slice-start
  1228.0 3.7 copy-start.13
  1228.0 7.1 slice-start.1
  1235.0 6.0 copy-start.1
Sparse Core Ops, SparseCore 0:
  10.0 132.9 all-gather.4
  144.9 68.7 all-gather.6
  264.5 35.7 all-gather.8
  302.7 36.7 all-gather.10
  360.5 51.3 reduce-scatter.9
  416.0 51.2 reduce-scatter.7
  476.9 71.4 reduce-scatter.13
  590.6 155.9 reduce-scatter.11
  750.0 34.2 reduce-scatter.15
  788.2 436.8 all-reduce.3
where the time goes:
time: 1250 us
  waiting for transfers between devices  879 us (70%)
  matrix products  145 us (12%)
  blocking collectives  92.4 us (7%)
  local copies, waits for them, and re-layouts  49.7 us (4%)
  other arithmetic  47.1 us (4%)
  between operations  15.2 us (1%)
  starting transfers between devices  13.4 us (1%)
    psum x1, waiting for transfers between devices, on_device(): lax.psum(mix_shard.astype(jnp.bfloat16), 'grp').astype(jnp.float32)  407 us
    reduce_scatter x1, waiting for transfers between devices, on_device(): lax.psum_scatter(mix_term.astype(jnp.bfloat16), 'seq', scatter_dimension=...  135 us
    all_gather x1, waiting for transfers between devices, on_device(): lax.all_gather(mix_weight, 'seq', axis=2, tiled=True)  121 us
    reduce_scatter x2, waiting for transfers between devices, summed_rows(): lax.psum_scatter(product(left).astype(jnp.bfloat16), 'seq', scatter_dimen...  98.3 us
    all_gather x2, waiting for transfers between devices, gather_rows(): return lax.all_gather(values, 'seq', axis=0, tiled=True)  61.5 us
    psum x1, blocking collectives, on_device(): lax.psum((jnp.stack([gain_one, gain_two]), jnp.stack([bias_one, bias_two]...  40.2 us
    all_to_all x1, waiting for transfers between devices, on_device(): lax.all_to_all(sending.reshape(slots_dev, 3, seq_count, local_width), 'se...  35.6 us
    all_to_all x1, blocking collectives, on_device(): lax.all_to_all(lowered, 'seq', split_axis=0, concat_axis=2, tiled=True)  29.5 us
  transfers between devices with their start and end apart: 13, of which 10 were waited for; matrix products, arithmetic and copies ran while one was open for 15% of the time, Pallas kernels for 0%

commit v1 on v0

--- a/solution.py
+++ b/solution.py
@@ -9,6 +9,35 @@
 EPS = 1e-05
 NEG = -1e30
 BASE = 10000.0
+
+
+def touch_bars_here(block_here):
+    q_next, current_block, part_next = (
+        lax.axis_size("seq"),
+        lax.axis_index("seq"),
+        block_here.shape[0],
+    )
+    rack = [(tick, (tick + 1) % q_next) for tick in range(q_next)]
+    panels = [(tick, (tick - 1) % q_next) for tick in range(q_next)]
+    spare = jnp.zeros(
+        (*block_here.shape[:0], q_next * part_next, *block_here.shape[1:]), block_here.dtype
+    )
+    spare = lax.dynamic_update_slice_in_dim(spare, block_here, current_block * part_next, axis=0)
+    field_out = w1 = block_here
+    r2 = q_next // 2
+    pp = 1
+    while pp < r2 + 1:
+        field_out = lax.ppermute(field_out, "seq", rack)
+        spare = lax.dynamic_update_slice_in_dim(
+            spare, field_out, (current_block - pp) % q_next * part_next, axis=0
+        )
+        if pp < q_next - r2:
+            w1 = lax.ppermute(w1, "seq", panels)
+            spare = lax.dynamic_update_slice_in_dim(
+                spare, w1, (current_block + pp) % q_next * part_next, axis=0
+            )
+        pp = pp + 1
+    return spare
 
 
 def layer_norm(values, gain, bias):
@@ -141,7 +170,7 @@
 
 
 def gather_rows(values):
-    return lax.all_gather(values, "seq", axis=0, tiled=True)
+    return touch_bars_here(values)
 
 
 def summed_rows(product, left):

time: 1250 us -> 1260 us (level)
  local copies, waits for them, and re-layouts: 49.7 us -> 66.2 us
  starting transfers between devices: 13.4 us -> 29.6 us
  waiting for transfers between devices: 879 us -> 864 us
    ppermute x0 -> x14, waiting for transfers between devices: none -> 84.8 us  [the longest x8 50.1 us: touch_bars_here(): field_out = lax.ppermute(field_out, 'seq', rack)]
    all_gather x2 -> x0, waiting for transfers between devices: 61.5 us -> none  [gather_rows(): return lax.all_gather(values, 'seq', axis=0, tiled=True)]
    all_to_all x1, waiting for transfers between devices: 35.6 us -> 0.01 us  [on_device(): lax.all_to_all(sending.reshape(slots_dev, 3, seq_count, local_width), 'se...]
    ppermute x0 -> x14, starting transfers between devices: none -> 16.3 us  [the longest x6 15.5 us: touch_bars_here(): w1 = lax.ppermute(w1, 'seq', panels)]
  transfers between devices with their start and end apart: 13 -> 25, of which waited for: 10 -> 16; matrix products, arithmetic and copies ran while one was open for 15% -> 15% of each run, Pallas kernels for 0% -> 0%
where the time goes in v1:
time: 1260 us
  waiting for transfers between devices  864 us (69%)
  matrix products  137 us (11%)
  blocking collectives  93.1 us (7%)
  local copies, waits for them, and re-layouts  66.2 us (5%)
  other arithmetic  44 us (3%)
  starting transfers between devices  29.6 us (2%)
  between operations  15.5 us (1%)
    psum x1, waiting for transfers between devices, on_device(): lax.psum(mix_shard.astype(jnp.bfloat16), 'grp').astype(jnp.float32)  407 us
    reduce_scatter x1, waiting for transfers between devices, on_device(): lax.psum_scatter(mix_term.astype(jnp.bfloat16), 'seq', scatter_dimension=...  135 us
    all_gather x1, waiting for transfers between devices, on_device(): lax.all_gather(mix_weight, 'seq', axis=2, tiled=True)  121 us
    reduce_scatter x2, waiting for transfers between devices, summed_rows(): lax.psum_scatter(product(left).astype(jnp.bfloat16), 'seq', scatter_dimen...  100 us
    ppermute x8, waiting for transfers between devices, touch_bars_here(): field_out = lax.ppermute(field_out, 'seq', rack)  50.1 us
    psum x1, blocking collectives, on_device(): lax.psum((jnp.stack([gain_one, gain_two]), jnp.stack([bias_one, bias_two]...  40.2 us
    ppermute x6, waiting for transfers between devices, touch_bars_here(): w1 = lax.ppermute(w1, 'seq', panels)  34.8 us
    all_to_all x1, blocking collectives, on_device(): lax.all_to_all(lowered, 'seq', split_axis=0, concat_axis=2, tiled=True)  30.7 us
  transfers between devices with their start and end apart: 25, of which 16 were waited for; matrix products, arithmetic and copies ran while one was open for 15% of the time, Pallas kernels for 0%

profile of v1, /device:TPU:0, one launch (start us, length us, event | category | flops | bytes accessed | tf_op | source)
XLA Modules:
  0.0 1256.1 jit_solution(14406550334248508599)
XLA Ops:
  9.5 10.4 all_gather.10
  21.9 121.0 %all-gather.3.cloned.1.call-done = bf16[2048,3,2048]{2,0,1:T(8,128)(2,1)} async-done(((bf16[2048,3,256]{2,0,1:T(8,128)(2,1)}), bf16[2048,3,2048]{2,0,1:T(8,128)(2,1)}) %all-gather.3.cloned.1.call-update) | async-done | bytes 25165840 | tf_op jit(solution)/shard_map/all_gather | solution.py:215
  143.0 13.4 %convolution_add_fusion = f32[128,3,2048]{2,0,1:T(8,128)} fusion(bf16[2048,3,2048]{2,0,1:T(8,128)(2,1)} %all-gather.3.cloned.1.call-done, f32[3,2048]{1,0:T(4,128)S(1)} %convert_element_type.139, bf16[128,2048]{1,0:T(8,128)(2,1)S(1)} %copy-done.5, f32[2048]{0:T(1024)S(1)} %bitcast.195, f32[2048]{0:T(1024)S(1)} %bitcast.191, f32[128]{0:T(128)S(1)} %add_rsqrt_fusion.1, ...), kind=kOutput, calls=%fused_computation.63 | convolution fusion | flops 3223584768 | bytes 28877824 | tf_op jit(solution)/shard_map/td,dcf->tcf/dot_general | solution.py:219
  156.4 3.5 copy.90
  164.7 4.4 all-to-all-start
  169.1 2.5 broadcast.289.clone.1
  175.5 47.8 %collective-permute-done.7 = bf16[128,2048]{1,0:T(8,128)(2,1)} collective-permute-done((bf16[128,2048]{1,0:T(8,128)(2,1)}, bf16[128,2048]{1,0:T(8,128)(2,1)}, u32[]{:S(2)}, u32[]{:S(2)}) %collective-permute-start.7) | collective-permute-done | bytes 524320 | tf_op jit(solution)/shard_map/ppermute | solution.py:30
  223.6 3.6 copy.92
  227.1 3.7 reshape.381
  230.8 2.5 slice_bitcast_fusion.6
  234.1 21.5 %while.27 = (s32[]{:T(128)}, bf16[2,512,4,64]{1,3,2,0:T(8,128)(2,1)}, f32[2,4,512]{2,1,0:T(4,128)S(1)}, s32[2]{0:T(128)S(1)}, s32[1024]{0:T(1024)S(1)}, /*index=...) while((s32[]{:T(128)}, ...), condition=%wide.region_10.11_spmd, body=%wide.region_7.10_spmd.sunk | while | flops 563608064 | bytes 35469596 | solution.py:118
  236.0 2.6 fusion.127
  238.7 2.3 fusion.128
  241.1 3.0 fusion.129
  246.8 2.6 fusion.127
  249.5 2.3 fusion.128
  251.8 3.0 fusion.129
  255.6 2.4 copy.93
  262.1 4.1 all-to-all-start.1
  266.4 2.6 collective-permute-start.10
  270.9 5.5 all-to-all-done.1
  276.5 4.9 fusion.82
  282.5 2.4 constant_dynamic-update-slice_fusion.5
  284.9 2.3 collective-permute-start.12
  289.1 2.6 collective-permute-start.1
  296.2 3.4 collective-permute-done.12
  300.4 10.3 collective-permute-done.1
  310.7 2.8 collective-permute-start.3
  315.3 9.7 collective-permute-done.3
  325.0 2.8 collective-permute-start.5
  328.5 11.4 collective-permute-done.5
  342.5 6.3 fusion.39
  348.8 7.5 fusion.45
  358.0 8.6 bitcast_convert_fusion
  367.1 6.4 convolution_convert_fusion.3
  373.5 46.7 %reduce-scatter.10.cloned.1.call-done = bf16[128,2048]{1,0:T(8,128)(2,1)} async-done(((bf16[1024,2048]{1,0:T(8,128)(2,1)}), bf16[128,2048]{1,0:T(8,128)(2,1)}) %reduce-scatter.10.cloned.1.call-update) | async-done | bytes 524304 | tf_op jit(solution)/shard_map/reduce_scatter | solution.py:177
  422.4 53.4 %reduce-scatter.8.cloned.1.call-done = bf16[128,2048]{1,0:T(8,128)(2,1)} async-done(((bf16[1024,2048]{1,0:T(8,128)(2,1)}), bf16[128,2048]{1,0:T(8,128)(2,1)}) %reduce-scatter.8.cloned.1.call-update) | async-done | bytes 524304 | tf_op jit(solution)/shard_map/reduce_scatter | solution.py:177
  475.8 2.3 fusion.63
  478.1 7.1 convolution_convert_fusion.1
  485.3 6.3 convolution_convert_fusion.5
  492.4 3.5 all-to-all-start.2
  496.1 9.4 all-to-all-done.2
  509.6 31.6 %while.28 = (s32[]{:T(128)}, f32[1024,4,64]{0,2,1:T(8,128)S(1)}, f32[1024,4,64]{0,2,1:T(8,128)}, bf16[2,512,4,64]{1,3,2,0:T(8,128)(2,1)}, s32[2]{0:T(128)S(1)}, ...) while((s32[]{:T(128)}, f32[1024,4,64]{0,2,1:T(8,128)S(1)}, ...), condition=%wide.region_19.20_spmd.clone, body=%wide.region_17.19_spmd.clone.sunk | while | flops 1376647680 | bytes 87103920 | solution.py:153
  514.8 2.5 fusion.142
  517.3 3.2 multiply_reduce_fusion.4
  520.5 2.4 multiply_convert_fusion.5
  530.6 2.6 fusion.142
  533.2 3.2 multiply_reduce_fusion.4
  536.3 2.4 multiply_convert_fusion.5
  544.9 2.9 copy.98
  547.8 30.7 %all_to_all.56 = bf16[1024,3,1,256]{3,1,2,0:T(4,128)(2,1)S(1)} all-to-all(bf16[1024,3,1,256]{3,1,2,0:T(4,128)(2,1)S(1)} %copy.98), channel_id=1, replica_groups=mesh['grp'=4,'seq'=8] {'seq'}, dimensions={0} | all-to-all | bytes 3145728 | tf_op jit(solution)/shard_map/all_to_all | solution.py:295
  586.8 11.9 convolution_convert_fusion
  598.8 10.8 convolution_convert_fusion.2
  611.3 8.9 convolution_convert_fusion.4
  620.1 134.7 %reduce-scatter.12.cloned.1.call-done = bf16[2048,3,256]{2,0,1:T(8,128)(2,1)} async-done(((bf16[2048,3,2048]{2,0,1:T(8,128)(2,1)}), bf16[2048,3,256]{2,0,1:T(8,128)(2,1)}) %reduce-scatter.12.cloned.1.call-update) | async-done | bytes 3145744 | tf_op jit(solution)/shard_map/reduce_scatter | solution.py:305
  754.9 14.6 %fusion.59 = (f32[2048]{0:T(1024)S(1)}, f32[128]{0:T(128)S(1)}, f32[128]{0:T(128)S(1)}, f32[2048]{0:T(1024)S(1)}, f32[128,2048]{1,0:T(8,128)}) fusion(bf16[128,2048]{1,0:T(8,128)(2,1)S(1)} %copy-done.6, f32[128]{0:T(128)S(1)} %copy-done.40, f32[128]{0:T(128)S(1)} %copy-done.38, f32[2048]{0:T(1024)S(1)} %bitcast.193, ...), kind=kOutput, calls=%fused_computation.93 | convolution fusion | flops 3225415680 | bytes 28338176 | tf_op jit(solution)/shard_map/tcf,dcf->td/dot_general | solution.py:301
  769.6 40.2 %all-reduce = (f32[2,2048]{1,0:T(2,128)}, f32[2,2048]{1,0:T(2,128)}) all-reduce(f32[2,2048]{1,0:T(2,128)S(1)} %pad_maximum_fusion.10, f32[2,2048]{1,0:T(2,128)S(1)} %pad_maximum_fusion.11), channel_id=1, replica_groups=mesh['grp'=4,'seq'=8] {'grp','seq'}, use_global_device_ids=true, to_apply=%region_24.25 | all-reduce | flops 8192 | bytes 65536 | tf_op jit(solution)/shard_map/psum | solution.py:324
  809.8 2.5 fusion.58
  813.2 11.9 psum.52
  825.7 407.2 %all-reduce.4.cloned.1.call-done = (bf16[2048,3,256]{2,0,1:T(8,128)(2,1)}, bf16[256,2048]{1,0:T(8,128)(2,1)}, bf16[2048,2,704]{0,2,1:T(8,128)(2,1)}, bf16[704,2048]{1,0:T(8,128)(2,1)}) async-done(((bf16[2048,3,256]{2,0,1:T(8,128)(2,1)}, bf16[256,2048]{1,0:T(8,128)(2,1)}, bf16[2048,2,704]{0,2,1:T(8,128)(2,1)}, bf16[704,2048]{1,0:T(8,128)(2,1)}), (bf16[2048,3,256]{2,0,1:T(8,128)(2,1)}, ...) | async-done | bytes 12845072 | tf_op jit(solution)/shard_map/psum | solution.py:318
  1232.9 2.9 convert_element_type.164
  1235.8 3.7 convert_element_type.161
  1239.5 3.3 convert_element_type.168
  1242.9 6.0 convert_element_type.166
  (269 shorter events, 71.9 us)
Async XLA Ops:
  7.2 341.6 %copy-start = (bf16[704,2048]{1,0:T(8,128)(2,1)S(1)}, bf16[704,2048]{1,0:T(8,128)(2,1)}, u32[]{:S(2)}) copy-start(bf16[704,2048]{1,0:T(8,128)(2,1)} %param.22) | copy-start | bytes 8650756
  7.2 2.3 copy-start.41
  7.2 12.8 %copy-start.5 = (bf16[128,2048]{1,0:T(8,128)(2,1)S(1)}, bf16[128,2048]{1,0:T(8,128)(2,1)}, u32[]{:S(2)}) copy-start(bf16[128,2048]{1,0:T(8,128)(2,1)} %param.15) | copy-start | bytes 1572868
  7.2 14.6 %copy-start.35 = (f32[2,2048]{1,0:T(2,128)S(1)}, f32[2,2048]{1,0:T(2,128)}, u32[]{:S(2)}) copy-start(f32[2,2048]{1,0:T(2,128)} %param.16) | copy-start | bytes 49156
  7.2 14.6 %copy-start.36 = (f32[2,2048]{1,0:T(2,128)S(1)}, f32[2,2048]{1,0:T(2,128)}, u32[]{:S(2)}) copy-start(f32[2,2048]{1,0:T(2,128)} %param.17) | copy-start | bytes 49156
  7.3 135.7 %all-gather.3.cloned.1.call-start = ((), (), s32[]{:S(2)}) async-start(), calls=%async_computation.9 | async-start | bytes 28311552 | tf_op jit(solution)/shard_map/all_gather | solution.py:215
  8.0 262.9 %all-gather.5.cloned.1.call-start = ((), (), s32[]{:S(2)}) async-start(), calls=%async_computation.10 | async-start | bytes 9437184 | tf_op jit(solution)/shard_map/all_gather | solution.py:217
  20.2 136.2 %copy-start.37 = (f32[128]{0:T(128)}, f32[128]{0:T(128)S(1)}, u32[]{:S(2)}) copy-start(f32[128]{0:T(128)S(1)} %broadcast_multiply_fusion.6) | copy-start | bytes 1540
  20.5 135.9 %copy-start.39 = (f32[128]{0:T(128)}, f32[128]{0:T(128)S(1)}, u32[]{:S(2)}) copy-start(f32[128]{0:T(128)S(1)} %add_rsqrt_fusion.1) | copy-start | bytes 1540
  21.9 141.2 %copy-start.30 = (f32[128,8]{0,1:T(8,128)}, f32[128,8]{0,1:T(8,128)S(1)}, u32[]{:S(2)}) copy-start(f32[128,8]{0,1:T(8,128)S(1)} %get-tuple-element.257) | copy-start | bytes 12292
  21.9 134.5 %copy-start.26 = (f32[1,2048]{1,0:T(1,128)}, f32[1,2048]{1,0:T(1,128)S(1)}, u32[]{:S(2)}) copy-start(f32[1,2048]{1,0:T(1,128)S(1)} %get-tuple-element.248) | copy-start | bytes 24580
  21.9 134.4 %copy-start.28 = (f32[1,2048]{1,0:T(1,128)}, f32[1,2048]{1,0:T(1,128)S(1)}, u32[]{:S(2)}) copy-start(f32[1,2048]{1,0:T(1,128)S(1)} %get-tuple-element.250) | copy-start | bytes 24580
  164.7 7.0 copy-start.21
  164.7 58.9 %all-to-all-start = ((bf16[128,3,8,256]{0,3,1,2:T(8,128)(2,1)}), bf16[128,3,8,256]{0,3,1,2:T(8,128)(2,1)}, u32[]{:S(2)}, u32[]{:S(2)}) async-start(bf16[128,3,8,256]{0,3,1,2:T(8,128)(2,1)} %copy.91), calls=%async_computation | async-start | bytes 3145728 | tf_op jit(solution)/shard_map/all_to_all | solution.py:231
  172.8 50.5 %collective-permute-start.7 = (bf16[128,2048]{1,0:T(8,128)(2,1)}, bf16[128,2048]{1,0:T(8,128)(2,1)}, u32[]{:S(2)}, u32[]{:S(2)}) collective-permute-start(bf16[128,2048]{1,0:T(8,128)(2,1)} %get-tuple-element.218), channel_id=1, source_target_pairs={{0,1},{1,2},{2,3},{3,4},{4,5},{5,6},{6,7},{7,0},{8,9},{9,10},{10,1... | collective-permute-start | bytes 1572872 | tf_op jit(solution)/shard_map/ppermute | solution.py:30
  173.2 93.2 %collective-permute-start.8 = (bf16[128,2048]{1,0:T(8,128)(2,1)}, bf16[128,2048]{1,0:T(8,128)(2,1)}, u32[]{:S(2)}, u32[]{:S(2)}) collective-permute-start(bf16[128,2048]{1,0:T(8,128)(2,1)} %get-tuple-element.218), channel_id=1, source_target_pairs={{0,7},{1,0},{2,1},{3,2},{4,3},{5,4},{6,5},{7,6},{8,15},{9,8},{10,9... | collective-permute-start | bytes 1572872 | tf_op jit(solution)/shard_map/ppermute | solution.py:35
  223.3 47.6 %collective-permute-start.9 = (bf16[128,2048]{1,0:T(8,128)(2,1)}, bf16[128,2048]{1,0:T(8,128)(2,1)}, u32[]{:S(2)}, u32[]{:S(2)}) collective-permute-start(bf16[128,2048]{1,0:T(8,128)(2,1)} %collective-permute-done.7), channel_id=1, source_target_pairs={{0,1},{1,2},{2,3},{3,4},{4,5},{5,6},{6,7},{7,0},{8,9},{9,10},{10,1... | collective-permute-start | bytes 1572872 | tf_op jit(solution)/shard_map/ppermute | solution.py:30
  238.7 2.4 copy-start.7
  238.7 2.4 copy-start.19
  249.4 2.4 copy-start.7
  249.4 2.4 copy-start.19
  262.1 14.4 %all-to-all-start.1 = ((bf16[8,128,256]{1,2,0:T(8,128)(2,1)}), bf16[8,128,256]{1,2,0:T(8,128)(2,1)}, u32[]{:S(2)}, u32[]{:S(2)}) async-start(bf16[8,128,256]{1,2,0:T(8,128)(2,1)} %copy.94), calls=%async_computation.1 | async-start | bytes 1048576 | tf_op jit(solution)/shard_map/all_to_all | solution.py:241
  266.2 154.0 %reduce-scatter.10.cloned.1.call-start = ((), (), s32[]{:S(2)}) async-start(), calls=%async_computation.12 | async-start | bytes 4718592 | tf_op jit(solution)/shard_map/reduce_scatter | solution.py:177
  266.4 18.5 %collective-permute-start.10 = (bf16[128,2048]{1,0:T(8,128)(2,1)}, bf16[128,2048]{1,0:T(8,128)(2,1)}, u32[]{:S(2)}, u32[]{:S(2)}) collective-permute-start(bf16[128,2048]{1,0:T(8,128)(2,1)} %collective-permute-done.8), channel_id=1, source_target_pairs={{0,7},{1,0},{2,1},{3,2},{4,3},{5,4},{6,5},{7,6},{8,15},{9,8},{10,9... | collective-permute-start | bytes 1572872 | tf_op jit(solution)/shard_map/ppermute | solution.py:35
  270.9 18.2 %collective-permute-start.11 = (bf16[128,2048]{1,0:T(8,128)(2,1)}, bf16[128,2048]{1,0:T(8,128)(2,1)}, u32[]{:S(2)}, u32[]{:S(2)}) collective-permute-start(bf16[128,2048]{1,0:T(8,128)(2,1)} %collective-permute-done.9), channel_id=1, source_target_pairs={{0,1},{1,2},{2,3},{3,4},{4,5},{5,6},{6,7},{7,0},{8,9},{9,10},{10,1... | collective-permute-start | bytes 1572872 | tf_op jit(solution)/shard_map/ppermute | solution.py:30
  281.4 3.5 copy-start.3
  281.7 60.8 %slice-start.2 = ((s8[5767168]{0:T(1024)(128)(4,1)}), s8[4194304]{0:T(1024)(128)(4,1)S(1)}, s32[]{:S(2)}) async-start(s8[5767168]{0:T(1024)(128)(4,1)} %bitcast.206), calls=%async_computation.19 | async-start | bytes 8388608
  282.5 11.8 collective-permute-start
  284.9 14.7 %collective-permute-start.12 = (bf16[128,2048]{1,0:T(8,128)(2,1)}, bf16[128,2048]{1,0:T(8,128)(2,1)S(1)}, u32[]{:S(2)}, u32[]{:S(2)}) collective-permute-start(bf16[128,2048]{1,0:T(8,128)(2,1)} %collective-permute-done.10), channel_id=1, source_target_pairs={{0,7},{1,0},{2,1},{3,2},{4,3},{5,4},{6,5},{7,6},{8,15},{9,8},{10,9... | collective-permute-start | bytes 1572872 | tf_op jit(solution)/shard_map/ppermute | solution.py:35
  289.1 24.4 %collective-permute-start.13 = (bf16[128,2048]{1,0:T(8,128)(2,1)}, bf16[128,2048]{1,0:T(8,128)(2,1)S(1)}, u32[]{:S(2)}, u32[]{:S(2)}) collective-permute-start(bf16[128,2048]{1,0:T(8,128)(2,1)} %collective-permute-done.11), channel_id=1, source_target_pairs={{0,1},{1,2},{2,3},{3,4},{4,5},{5,6},{6,7},{7,0},{8,9},{9,10},{10,1... | collective-permute-start | bytes 1572872 | tf_op jit(solution)/shard_map/ppermute | solution.py:30
  289.1 21.6 %collective-permute-start.1 = (bf16[128,2048]{1,0:T(8,128)(2,1)S(1)}, bf16[128,2048]{1,0:T(8,128)(2,1)S(1)}, u32[]{:S(2)}, u32[]{:S(2)}) collective-permute-start(bf16[128,2048]{1,0:T(8,128)(2,1)S(1)} %get-tuple-element.220), channel_id=1, source_target_pairs={{0,7},{1,0},{2,1},{3,2},{4,3},{5,4},{6,5},{7,6},{8,15},{9,8},{10,9... | collective-permute-start | bytes 1572872 | tf_op jit(solution)/shard_map/ppermute | solution.py:35
  293.6 48.9 %slice-start.3 = ((s8[5767168]{0:T(1024)(128)(4,1)}), s8[1572864]{0:T(1024)(128)(4,1)S(1)}, s32[]{:S(2)}) async-start(s8[5767168]{0:T(1024)(128)(4,1)} %bitcast.206), calls=%async_computation.20 | async-start | bytes 3145728
  294.3 20.9 %collective-permute-start.2 = (bf16[128,2048]{1,0:T(8,128)(2,1)S(1)}, bf16[128,2048]{1,0:T(8,128)(2,1)S(1)}, u32[]{:S(2)}, u32[]{:S(2)}) collective-permute-start(bf16[128,2048]{1,0:T(8,128)(2,1)S(1)} %collective-permute-done), channel_id=1, source_target_pairs={{0,1},{1,2},{2,3},{3,4},{4,5},{5,6},{6,7},{7,0},{8,9},{9,10},{10,1... | collective-permute-start | bytes 1572872 | tf_op jit(solution)/shard_map/ppermute | solution.py:30
  310.7 14.3 %collective-permute-start.3 = (bf16[128,2048]{1,0:T(8,128)(2,1)S(1)}, bf16[128,2048]{1,0:T(8,128)(2,1)S(1)}, u32[]{:S(2)}, u32[]{:S(2)}) collective-permute-start(bf16[128,2048]{1,0:T(8,128)(2,1)S(1)} %collective-permute-done.1), channel_id=1, source_target_pairs={{0,7},{1,0},{2,1},{3,2},{4,3},{5,4},{6,5},{7,6},{8,15},{9,8},{10,9... | collective-permute-start | bytes 1572872 | tf_op jit(solution)/shard_map/ppermute | solution.py:35
  315.2 12.9 %collective-permute-start.4 = (bf16[128,2048]{1,0:T(8,128)(2,1)S(1)}, bf16[128,2048]{1,0:T(8,128)(2,1)S(1)}, u32[]{:S(2)}, u32[]{:S(2)}) collective-permute-start(bf16[128,2048]{1,0:T(8,128)(2,1)S(1)} %collective-permute-done.2), channel_id=1, source_target_pairs={{0,1},{1,2},{2,3},{3,4},{4,5},{5,6},{6,7},{7,0},{8,9},{9,10},{10,1... | collective-permute-start | bytes 1572872 | tf_op jit(solution)/shard_map/ppermute | solution.py:30
  325.0 14.9 %collective-permute-start.5 = (bf16[128,2048]{1,0:T(8,128)(2,1)S(1)}, bf16[128,2048]{1,0:T(8,128)(2,1)S(1)}, u32[]{:S(2)}, u32[]{:S(2)}) collective-permute-start(bf16[128,2048]{1,0:T(8,128)(2,1)S(1)} %collective-permute-done.3), channel_id=1, source_target_pairs={{0,7},{1,0},{2,1},{3,2},{4,3},{5,4},{6,5},{7,6},{8,15},{9,8},{10,9... | collective-permute-start | bytes 1572872 | tf_op jit(solution)/shard_map/ppermute | solution.py:35
  328.1 12.3 collective-permute-start.6
  340.4 2.0 copy-start.14
  366.5 109.2 %reduce-scatter.8.cloned.1.call-start = ((), (), s32[]{:S(2)}) async-start(), calls=%async_computation.11 | async-start | bytes 4718592 | tf_op jit(solution)/shard_map/reduce_scatter | solution.py:177
  373.5 46.8 %copy-start.4 = (f32[128,2048]{1,0:T(8,128)S(1)}, f32[128,2048]{1,0:T(8,128)}, u32[]{:S(2)}) copy-start(f32[128,2048]{1,0:T(8,128)} %copy-done.3) | copy-start | bytes 3145732
  373.5 102.3 %copy-start.22 = (bf16[128,2048]{1,0:T(8,128)(2,1)S(1)}, bf16[128,2048]{1,0:T(8,128)(2,1)}, u32[]{:S(2)}) copy-start(bf16[128,2048]{1,0:T(8,128)(2,1)} %param.25) | copy-start | bytes 1572868
  373.5 246.7 %reduce-scatter.14.cloned.1.call-start = ((), (), s32[]{:S(2)}) async-start(), calls=%async_computation.14 | async-start | bytes 9437184 | tf_op jit(solution)/shard_map/reduce_scatter | solution.py:311
  478.1 7.2 copy-start.9
  491.5 18.0 %copy-start.2 = (bf16[1024,4,64]{0,2,1:T(8,128)(2,1)S(1)}, bf16[1024,4,64]{0,2,1:T(8,128)(2,1)}, u32[]{:S(2)}) copy-start(bf16[1024,4,64]{0,2,1:T(8,128)(2,1)} %get-tuple-element.492) | copy-start | bytes 1572868
  491.6 18.0 %copy-start.8 = (bf16[1024,4,64]{0,2,1:T(8,128)(2,1)S(1)}, bf16[1024,4,64]{0,2,1:T(8,128)(2,1)}, u32[]{:S(2)}) copy-start(bf16[1024,4,64]{0,2,1:T(8,128)(2,1)} %get-tuple-element.493) | copy-start | bytes 1572868
  492.4 13.2 %all-to-all-start.2 = ((bf16[128,8,256]{2,0,1:T(8,128)(2,1)}), bf16[128,8,256]{2,0,1:T(8,128)(2,1)S(1)}, u32[]{:S(2)}, u32[]{:S(2)}) async-start(bf16[128,8,256]{2,0,1:T(8,128)(2,1)} %bitcast.142), calls=%async_computation.4 | async-start | bytes 1048576 | tf_op jit(solution)/shard_map/all_to_all | solution.py:284
  495.9 259.0 %reduce-scatter.12.cloned.1.call-start = ((), (), s32[]{:S(2)}) async-start(), calls=%async_computation.13 | async-start | bytes 28311552 | tf_op jit(solution)/shard_map/reduce_scatter | solution.py:305
  517.3 3.2 copy-start.24
  520.5 2.4 copy-start.17
  533.1 3.2 copy-start.24
  536.3 2.4 copy-start.17
  541.2 2.3 copy-start.25
  583.4 2.4 copy-start.31
  583.4 2.4 copy-start.34
  598.7 213.5 %reduce-scatter.16.cloned.1.call-start = ((), (), s32[]{:S(2)}) async-start(), calls=%async_computation.15 | async-start | bytes 589824
  611.0 621.9 %all-reduce.4.cloned.1.call-start = ((), (), s32[]{:S(2)}) async-start(), calls=%async_computation.16 | async-start | bytes 25690112 | tf_op jit(solution)/shard_map/psum | solution.py:318
  754.9 14.7 %copy-start.33 = (f32[2048]{0:T(1024)S(1)}, f32[2048]{0:T(1024)}, u32[]{:S(2)}) copy-start(f32[2048]{0:T(1024)} %get-tuple-element.165) | copy-start | bytes 24580
  754.9 14.7 %copy-start.32 = (f32[2048]{0:T(1024)S(1)}, f32[2048]{0:T(1024)}, u32[]{:S(2)}) copy-start(f32[2048]{0:T(1024)} %get-tuple-element.170) | copy-start | bytes 24580
  754.9 54.9 %copy-start.10 = (f32[128,2048]{1,0:T(8,128)S(1)}, f32[128,2048]{1,0:T(8,128)}, u32[]{:S(2)}) copy-start(f32[128,2048]{1,0:T(8,128)} %copy-done.9) | copy-start | bytes 3145732
  1232.9 2.9 copy-start.15
  1232.9 10.0 slice-start
  1235.8 3.7 copy-start.16
  1235.8 7.1 slice-start.1
  1242.9 6.0 copy-start.1
  (19 other events, 23.0 us)
Sparse Core Ops, SparseCore 0:
  10.0 132.9 all-gather.2
  144.9 76.6 all-gather.4
  366.7 53.5 reduce-scatter.9
  424.4 51.3 reduce-scatter.7
  485.4 73.0 reduce-scatter.13
  598.9 155.9 reduce-scatter.11
  758.2 34.2 reduce-scatter.15
  796.0 436.8 all-reduce.3
